TPU v7x, 256 devices: a whole 4x4x8 slice. The times are simulated.
256 devices in a mesh: ga: 16 (over z_lo, y), pair: 16 (over z_hi, x, core).
Axes of the slice: x: 4, y: 4, z: 8 (z_hi: 2, z_lo: 4; z = z_hi * 4 + z_lo), core: 2. Of those that a mesh axis runs over, the one named last changes fastest.
Arguments:
- val_density: bfloat16 [256, 3, 2, 8192], P('pair', None, None, 'ga'), may hold values from -0.0625 to 0.0625
- con_density: bfloat16 [576, 3, 2, 8192], P('ga', None, None, 'pair'), may hold values from -6 to 6
- screened: bfloat16 [3, 2, 8192, 8192], P(None, None, 'ga', 'pair'), may hold values from -0.0625 to 0.0625
- coulomb: float32 [3, 8192], P(None, 'ga'), may hold values from 0.2 to 2
- trans_here: bfloat16 [384, 2, 8192], P('pair', None, 'ga'), may hold values from -6 to 6
- trans_there: bfloat16 [384, 3, 2, 8192], P('pair', None, None, 'ga'), may hold values from -0.0625 to 0.0625
- shift_map: int32 [3, 8192], P(None, 'pair'), may hold values from 0 to 8191, as said below
- ordering: int32 [384], replicated, may hold values from 0 to 383, each once
Outputs:
- kernel: float32 [3, 2, 384, 384], P(None, None, 'pair', 'ga')
Inputs may be any that keep to these rules, and one draw needn't show every extreme that they name: `shift_map`: each aligned block of 128 entries of a row is a permutation of that block's own G-vector indices.
All inputs are finite; a program needn't handle non-finite values.
Results may differ from a plain program's by a relative error of at most 0.0003.
Values may be sent and summed in bfloat16 or wider, within the bound.
A program may use at most 64 MiB of HBM per device.

v0:
```python
import jax
import jax.numpy as jnp
from jax import lax
from jax.sharding import PartitionSpec as P

NV = 16
NC = 24
GBLK = 128
NT = 384


def contract_float(left, right):
    high = lax.Precision.HIGHEST
    real_part = jnp.einsum(
        "nkg,mkg->nkm", left[:, :, 0], right[:, :, 0], precision=high
    ) - jnp.einsum("nkg,mkg->nkm", left[:, :, 1], right[:, :, 1], precision=high)
    imag_part = jnp.einsum(
        "nkg,mkg->nkm", left[:, :, 0], right[:, :, 1], precision=high
    ) + jnp.einsum("nkg,mkg->nkm", left[:, :, 1], right[:, :, 0], precision=high)
    return jnp.stack([real_part, imag_part], axis=2)


def times_cols(rows, weights):
    first = jnp.einsum(
        "nkh,kgh->nkg", rows[:, :, 0], weights[:, 0], preferred_element_type=jnp.float32
    ) - jnp.einsum("nkh,kgh->nkg", rows[:, :, 1], weights[:, 1], preferred_element_type=jnp.float32)
    second = jnp.einsum(
        "nkh,kgh->nkg", rows[:, :, 0], weights[:, 1], preferred_element_type=jnp.float32
    ) + jnp.einsum("nkh,kgh->nkg", rows[:, :, 1], weights[:, 0], preferred_element_type=jnp.float32)
    return jnp.stack([first, second], axis=2)


def on_device(
    val_density, con_density, screened, coulomb, trans_here, trans_there, shift_map, ordering
):
    con_count = con_density.shape[0]
    points = con_density.shape[1]
    slab_cols = con_density.shape[3]
    blocks = slab_cols // GBLK
    within = (shift_map % GBLK).reshape(points, blocks, GBLK)
    onehot = (
        within[:, :, :, None] == jnp.arange(GBLK, dtype=jnp.int32)[None, None, None, :]
    ).astype(jnp.bfloat16)
    con_blocks = con_density.reshape(con_count, points, 2, blocks, GBLK)
    shifted = (
        jnp.einsum("bkpnh,kngh->bkpng", con_blocks, onehot, preferred_element_type=jnp.float32)
        .astype(jnp.bfloat16)
        .reshape(con_density.shape)
    )
    whole_here = lax.all_gather(trans_here, "pair", axis=0, tiled=True).astype(jnp.float32)
    weighted = trans_there.astype(jnp.float32) * coulomb[None, :, None, :]
    high = lax.Precision.HIGHEST
    exch_real = jnp.einsum(
        "tg,skg->tks", whole_here[:, 0], weighted[:, :, 0], precision=high
    ) - jnp.einsum("tg,skg->tks", whole_here[:, 1], weighted[:, :, 1], precision=high)
    exch_imag = jnp.einsum(
        "tg,skg->tks", whole_here[:, 0], weighted[:, :, 1], precision=high
    ) + jnp.einsum("tg,skg->tks", whole_here[:, 1], weighted[:, :, 0], precision=high)
    exch_part = jnp.stack([exch_real, exch_imag], axis=2)
    whole_con = lax.all_gather(shifted, "ga", axis=0, tiled=True)
    screened_rows = lax.psum_scatter(
        times_cols(whole_con, screened), "pair", scatter_dimension=0, tiled=True
    )
    direct_part = contract_float(
        lax.all_gather(val_density, "pair", axis=0, tiled=True).astype(jnp.float32), screened_rows
    )
    direct_sum, exch_sum = lax.psum((direct_part, exch_part), "ga")
    direct_full, exch_full = (
        lax.all_gather(direct_sum, "pair", axis=3, tiled=True),
        lax.all_gather(exch_sum, "pair", axis=3, tiled=True),
    )
    row_count = NT // lax.axis_size("pair")
    col_count = NT // lax.axis_size("ga")
    row_trans = lax.dynamic_slice_in_dim(ordering, lax.axis_index("pair") * row_count, row_count, 0)
    col_trans = lax.dynamic_slice_in_dim(ordering, lax.axis_index("ga") * col_count, col_count, 0)
    row_pairs = (row_trans // NC)[:, None] * NV + (col_trans // NC)[None, :]
    col_pairs = (row_trans % NC)[:, None] * NC + (col_trans % NC)[None, :]
    picked = direct_full[row_pairs.reshape(-1)]
    col_mask = (
        col_pairs.reshape(-1)[:, None] == jnp.arange(direct_full.shape[3], dtype=jnp.int32)[None, :]
    ).astype(jnp.float32)
    direct_flat = jnp.sum(picked * col_mask[:, None, None, :], axis=3)
    direct_sel = jnp.transpose(direct_flat.reshape(row_count, col_count, points, 2), (2, 3, 0, 1))
    exch_picked = exch_full[row_trans]
    col_hot = (jnp.arange(NT, dtype=jnp.int32)[:, None] == col_trans[None, :]).astype(jnp.float32)
    exch_sel = jnp.einsum("rkpt,tc->kprc", exch_picked, col_hot, precision=high)
    return 2.0 * exch_sel - direct_sel


def solution(mesh):
    in_specs = (
        P("pair", None, None, "ga"),
        P("ga", None, None, "pair"),
        P(None, None, "ga", "pair"),
        P(None, "ga"),
        P("pair", None, "ga"),
        P("pair", None, None, "ga"),
        P(None, "pair"),
        P(),
    )
    out_specs = P(None, None, "pair", "ga")
    return jax.shard_map(
        on_device, mesh=mesh, in_specs=in_specs, out_specs=out_specs, check_vma=False
    )
```

profile of v0, /device:TPU:1, one launch (start us, length us, event | category | flops | bytes accessed | tf_op | source)
XLA Modules:
  0.0 732.0 jit_solution(17700112051085489857)
XLA Ops:
  6.5 0.0 all-gather.7.cloned.1.call-start
  6.5 1.1 reshape.80
  7.6 0.7 add_select_fusion
  8.3 0.5 fusion.11
  8.8 0.1 copy.35
  8.9 0.8 reshape.81
  9.7 0.0 all-gather.7.cloned.1.call-update
  9.7 0.0 copy-start
  9.7 0.0 all-reduce.5.cloned.1.call-start
  9.8 80.6 %all-gather.7.cloned.1.call-done = bf16[576,3,2,512]{3,2,1,0:T(2,128)(2,1)} async-done(((bf16[36,3,2,512]{3,2,1,0:T(2,128)(2,1)}), bf16[576,3,2,512]{3,2,1,0:T(2,128)(2,1)}) %all-gather.7.cloned.1.call-update) | async-done | bytes 3538960 | tf_op jit(solution)/shard_map/all_gather | solution.py:60
  90.4 9.1 %fusion.34 = (bf16[576,3,1,512]{3,2,1,0:T(2,128)(2,1)S(1)}, bf16[576,3,1,512]{3,2,1,0:T(2,128)(2,1)S(1)}) fusion(bf16[576,3,2,512]{3,2,1,0:T(2,128)(2,1)} %all-gather.7.cloned.1.call-done), kind=kLoop, calls=%fused_computation.75 | loop fusion | bytes 7077888 | tf_op jit(solution)/shard_map/slice | solution.py:26
  99.5 0.0 copy-done
  99.5 1.1 fusion.4
  100.6 1.1 fusion
  101.8 1.2 subtract_bitcast_fusion
  102.9 1.2 add_bitcast_fusion
  104.1 3.8 pad_maximum_fusion
  107.9 11.3 %copy.40 = f32[576,3,2,512]{3,2,1,0:T(2,128)} copy(f32[576,3,2,512]{3,0,1,2:T(8,128)} %pad_maximum_fusion) | data formatting | bytes 14155776 | tf_op jit(solution)/shard_map/stack | solution.py:30
  119.2 0.0 copy-start.5
  119.3 0.0 all-reduce.5.cloned.1.call-update
  119.3 0.0 all-gather.9.cloned.1.call-start
  119.3 0.8 copy-done.3
  120.1 0.6 copy.42
  120.8 0.0 all-gather.9.cloned.1.call-update
  120.8 0.0 all-reduce.7.cloned.1.call-start
  120.9 0.6 dynamic-slice
  122.2 47.9 %all_gather.15 = bf16[384,2,512]{2,0,1:T(8,128)(2,1)S(1)} all-gather(bf16[24,2,512]{2,0,1:T(8,128)(2,1)S(1)} %copy.31), channel_id=1, replica_groups=mesh['ga'=16,'pair'=16] {'pair'}, dimensions={0}, use_global_device_ids=true | all-gather | bytes 835584 | tf_op jit(solution)/shard_map/all_gather | solution.py:50
  170.1 0.5 fusion.24
  170.6 0.5 fusion.15
  171.1 0.5 fusion.23
  171.6 0.5 fusion.14
  172.1 0.7 pad_maximum_fusion.2
  172.8 168.5 %all-reduce.5.cloned.1.call-done = f32[576,3,2,512]{3,2,1,0:T(2,128)} async-done(((f32[576,3,2,512]{3,2,1,0:T(2,128)}), f32[576,3,2,512]{3,2,1,0:T(2,128)}) %all-reduce.5.cloned.1.call-update) | async-done | bytes 7077904
  341.3 1.5 constant_dynamic-slice_fusion
  342.8 0.0 copy-start.6
  342.8 64.9 %all-gather.9.cloned.1.call-done = bf16[256,3,2,512]{3,0,1,2:T(8,128)(2,1)} async-done(((bf16[16,3,2,512]{3,0,1,2:T(8,128)(2,1)}), bf16[256,3,2,512]{3,0,1,2:T(8,128)(2,1)}) %all-gather.9.cloned.1.call-update) | async-done | bytes 1572880 | tf_op jit(solution)/shard_map/all_gather | solution.py:65
  407.7 2.0 fusion.21
  409.7 1.9 fusion.20
  411.7 1.9 fusion.13
  413.6 0.0 copy-done.1
  413.6 0.8 fusion.12
  414.4 0.7 pad_maximum_fusion.1
  415.1 0.0 all-reduce.7.cloned.1.call-update
  415.1 0.0 all-gather.11.cloned.1.call-start
  415.2 146.2 %all-reduce.7.cloned.1.call-done = (f32[384,3,2,24]{0,3,1,2:T(8,128)}, f32[256,3,2,36]{0,3,1,2:T(8,128)}) async-done(((f32[384,3,2,24]{0,3,1,2:T(8,128)}, f32[256,3,2,36]{0,3,1,2:T(8,128)}), (f32[384,3,2,24]{0,3,1,2:T(8,128)}, f32[256,3,2,36]{0,3,1,2:T(8,128)})) %all-reduce.7.cloned.1.call-update) | async-done | bytes 442384 | tf_op jit(solution)/shard_map/psum | solution.py:67
  561.3 1.8 copy.44
  563.1 0.0 all-gather.11.cloned.1.call-update
  563.1 0.0 all-gather.5.cloned.1.call-start
  563.2 0.5 all-gather.5.cloned.1.call-update
  563.7 0.1 fusion.32
  563.8 0.1 broadcast_add_fusion
  563.9 0.1 add.121
  564.0 0.1 add.129
  564.1 0.2 fusion.6
  564.3 80.0 %all-gather.11.cloned.1.call-done = f32[256,3,2,576]{0,2,1,3:T(2,128)} async-done(((f32[256,3,2,36]{0,2,1,3:T(2,128)}), f32[256,3,2,576]{0,2,1,3:T(2,128)}) %all-gather.11.cloned.1.call-update) | async-done | bytes 3538960 | tf_op jit(solution)/shard_map/all_gather | solution.py:69
  644.3 8.0 %copy.45 = f32[256,3,2,576]{3,2,1,0:T(2,128)} copy(f32[256,3,2,576]{0,2,1,3:T(2,128)} %all-gather.11.cloned.1.call-done) | data formatting | bytes 7077888 | tf_op jit(solution)/shard_map/all_gather | solution.py:69
  652.4 25.7 %gather_fusion.1 = f32[576,3,2,576]{3,2,1,0:T(2,128)} fusion(f32[256,3,2,576]{3,2,1,0:T(2,128)} %copy.45, s32[1024]{0:T(1024)S(1)} %pad_clamp_fusion), kind=kCustom, calls=%fused_computation.1 | custom fusion | bytes 15927552 | tf_op jit(solution)/shard_map/gather | solution.py:78
  678.1 6.7 multiply_reduce_fusion
  684.8 1.2 copy.47
  686.0 29.2 %all-gather.5.cloned.1.call-done = f32[384,3,2,384]{0,3,1,2:T(8,128)} async-done(((f32[384,3,2,24]{0,3,1,2:T(8,128)}), f32[384,3,2,384]{0,3,1,2:T(8,128)}) %all-gather.5.cloned.1.call-update) | async-done | bytes 3538960 | tf_op jit(solution)/shard_map/all_gather | solution.py:70
  715.3 6.2 copy.32
  721.5 1.5 gather_fusion
  722.9 1.5 fusion.17
  724.5 0.7 copy.48
  (17 shorter events, 0.1 us)
Async XLA Ops:
  6.5 83.9 %all-gather.7.cloned.1.call-start = ((), (), s32[]{:S(2)}) async-start(), calls=%async_computation.1 | async-start | bytes 3760128 | tf_op jit(solution)/shard_map/all_gather | solution.py:60
  9.7 89.8 %copy-start = (bf16[3,2,512,512]{3,2,1,0:T(8,128)(2,1)S(1)}, bf16[3,2,512,512]{3,2,1,0:T(8,128)(2,1)}, u32[]{:S(2)}) copy-start(bf16[3,2,512,512]{3,2,1,0:T(8,128)(2,1)} %param.10) | copy-start | bytes 9437188
  9.7 331.5 %all-reduce.5.cloned.1.call-start = ((), (), s32[]{:S(2)}) async-start(), calls=%async_computation.4 | async-start | bytes 14155776
  119.2 0.9 copy-start.3
  119.2 1.6 copy-start.4
  119.2 1.7 copy-start.7
  119.2 2.9 copy-start.2
  119.2 2.9 copy-start.5
  119.3 288.4 %all-gather.9.cloned.1.call-start = ((), (), s32[]{:S(2)}) async-start(), calls=%async_computation.2 | async-start | bytes 1671168 | tf_op jit(solution)/shard_map/all_gather | solution.py:65
  120.8 440.5 %all-reduce.7.cloned.1.call-start = ((), (), s32[]{:S(2)}) async-start(), calls=%async_computation.5 | async-start | bytes 933888 | tf_op jit(solution)/shard_map/psum | solution.py:67
  342.8 220.9 %copy-start.6 = (s32[384]{0:T(512)S(1)}, s32[384]{0:T(512)}, u32[]{:S(2)}) copy-start(s32[384]{0:T(512)} %param.15) | copy-start | bytes 4612
  407.7 5.9 copy-start.1
  415.1 229.2 %all-gather.11.cloned.1.call-start = ((), (), s32[]{:S(2)}) async-start(), calls=%async_computation.3 | async-start | bytes 3760128 | tf_op jit(solution)/shard_map/all_gather | solution.py:69
  563.1 152.2 %all-gather.5.cloned.1.call-start = ((), (), s32[]{:S(2)}) async-start(), calls=%async_computation | async-start | bytes 3760128 | tf_op jit(solution)/shard_map/all_gather | solution.py:70
Sparse Core Ops, SparseCore 0:
  9.8 80.5 all-gather.6
  119.4 221.8 all-reduce.4
  344.1 63.5 all-gather.8
  415.2 146.0 all-reduce.6
  563.9 80.4 all-gather.10
  646.9 68.3 all-gather.4
where the time goes:
time: 733 us; the launch traced here: 732 us
  waiting for transfers between devices  570 us (78%)
  local copies, waits for them, and re-layouts  71.3 us (10%)
  blocking collectives  47.9 us (7%)
  matrix products  15.1 us (2%)
  between operations  14.4 us (2%)
  other arithmetic  13 us (2%)
    unnamed x7, waiting for transfers between devices  169 us
    psum x1, waiting for transfers between devices, on_device(): direct_sum, exch_sum = lax.psum((direct_part, exch_part), 'ga')  146 us
    all_gather x1, waiting for transfers between devices, on_device(): whole_con = lax.all_gather(shifted, 'ga', axis=0, tiled=True)  80.6 us
    all_gather x1, waiting for transfers between devices, on_device(): lax.all_gather(direct_sum, 'pair', axis=3, tiled=True)  80 us
    all_gather x1, waiting for transfers between devices, on_device(): lax.all_gather(val_density, 'pair', axis=0, tiled=True).astype(jnp.float32)  64.9 us
    all_gather x1, blocking collectives, on_device(): lax.all_gather(trans_here, 'pair', axis=0, tiled=True).astype(jnp.float32)  47.9 us
    all_gather x1, waiting for transfers between devices, on_device(): lax.all_gather(exch_sum, 'pair', axis=3, tiled=True)  29.2 us
    gather x1, local copies, waits for them, and re-layouts, on_device(): picked = direct_full[row_pairs.reshape(-1)]  25.7 us
  transfers between devices with their start and end apart: 6, of which 6 were waited for; matrix products, arithmetic and copies ran while one was open for 7% of the time, Pallas kernels for 0%

commit v1 on v0

--- a/solution.py
+++ b/solution.py
@@ -66,7 +66,9 @@
     )
     direct_sum, exch_sum = lax.psum((direct_part, exch_part), "ga")
     direct_full, exch_full = (
-        lax.all_gather(direct_sum, "pair", axis=3, tiled=True),
+        jnp.concatenate(
+            lax.all_to_all(jnp.stack([direct_sum] * lax.axis_size("pair")), "pair", 0, 0), axis=3
+        ),
         lax.all_gather(exch_sum, "pair", axis=3, tiled=True),
     )
     row_count = NT // lax.axis_size("pair")

time: 733 us -> 759 us (1.035); the launches traced: 732 us -> 749 us
  starting transfers between devices: 0.21 us -> 19 us
  waiting for transfers between devices: 570 us -> 556 us
  local copies, waits for them, and re-layouts: 71.3 us -> 79.1 us
    all_to_all x0 -> x1, waiting for transfers between devices: none -> 93.6 us  [on_device(): lax.all_to_all(jnp.stack([direct_sum] * lax.axis_size('pair')), 'pair', 0...]
    all_gather x1 -> x0, waiting for transfers between devices: 80 us -> none  [on_device(): lax.all_gather(direct_sum, 'pair', axis=3, tiled=True)]
    all_gather x1, waiting for transfers between devices: 29.2 us -> 0.01 us  [on_device(): lax.all_gather(exch_sum, 'pair', axis=3, tiled=True)]
    all_to_all x0 -> x1, starting transfers between devices: none -> 18.8 us  [on_device(): lax.all_to_all(jnp.stack([direct_sum] * lax.axis_size('pair')), 'pair', 0...]
    reshape x0 -> x2, local copies, waits for them, and re-layouts: none -> 11.3 us  [on_device(): jnp.concatenate(lax.all_to_all(jnp.stack([direct_sum] * lax.axis_size('pa...]
    all_gather x1 -> x0, local copies, waits for them, and re-layouts: 8.04 us -> none  [on_device(): lax.all_gather(direct_sum, 'pair', axis=3, tiled=True)]
    unnamed x7 -> x6, waiting for transfers between devices: 169 us -> 171 us
  transfers between devices with their start and end apart: 6 -> 6, of which waited for: 6 -> 5; matrix products, arithmetic and copies ran while one was open for 7% -> 8% of each run, Pallas kernels for 0% -> 0%
where the time goes in v1:
time: 759 us; the launch traced here: 749 us
  waiting for transfers between devices  556 us (73%)
  local copies, waits for them, and re-layouts  79.1 us (10%)
  blocking collectives  47.9 us (6%)
  starting transfers between devices  19 us (3%)
  other arithmetic  17.2 us (2%)
  matrix products  15.1 us (2%)
  between operations  14.1 us (2%)
    unnamed x6, waiting for transfers between devices  171 us
    psum x1, waiting for transfers between devices, on_device(): direct_sum, exch_sum = lax.psum((direct_part, exch_part), 'ga')  146 us
    all_to_all x1, waiting for transfers between devices, on_device(): lax.all_to_all(jnp.stack([direct_sum] * lax.axis_size('pair')), 'pair', 0...  93.6 us
    all_gather x1, waiting for transfers between devices, on_device(): whole_con = lax.all_gather(shifted, 'ga', axis=0, tiled=True)  80.6 us
    all_gather x1, waiting for transfers between devices, on_device(): lax.all_gather(val_density, 'pair', axis=0, tiled=True).astype(jnp.float32)  64.8 us
    all_gather x1, blocking collectives, on_device(): lax.all_gather(trans_here, 'pair', axis=0, tiled=True).astype(jnp.float32)  47.9 us
    gather x1, local copies, waits for them, and re-layouts, on_device(): picked = direct_full[row_pairs.reshape(-1)]  26.6 us
    all_to_all x1, starting transfers between devices, on_device(): lax.all_to_all(jnp.stack([direct_sum] * lax.axis_size('pair')), 'pair', 0...  18.8 us
  transfers between devices with their start and end apart: 6, of which 5 were waited for; matrix products, arithmetic and copies ran while one was open for 8% of the time, Pallas kernels for 0%

profile of v1, /device:TPU:1, one launch (start us, length us, event | category | flops | bytes accessed | tf_op | source)
XLA Modules:
  0.0 748.5 jit_solution(1961435452112081598)
XLA Ops:
  6.5 0.0 all-gather.6.cloned.1.call-start
  6.5 0.7 add_select_fusion
  7.3 1.1 reshape.88
  8.3 0.5 fusion.11
  8.8 0.1 copy.50
  8.9 0.8 reshape.89
  9.7 0.0 all-gather.6.cloned.1.call-update
  9.7 0.0 copy-start
  9.7 0.0 all-reduce.5.cloned.1.call-start
  9.8 80.6 %all-gather.6.cloned.1.call-done = bf16[576,3,2,512]{3,2,1,0:T(2,128)(2,1)} async-done(((bf16[36,3,2,512]{3,2,1,0:T(2,128)(2,1)}), bf16[576,3,2,512]{3,2,1,0:T(2,128)(2,1)}) %all-gather.6.cloned.1.call-update) | async-done | bytes 3538960 | tf_op jit(solution)/shard_map/all_gather | solution.py:60
  90.4 9.1 %fusion.34 = (bf16[576,3,1,512]{3,2,1,0:T(2,128)(2,1)S(1)}, bf16[576,3,1,512]{3,2,1,0:T(2,128)(2,1)S(1)}) fusion(bf16[576,3,2,512]{3,2,1,0:T(2,128)(2,1)} %all-gather.6.cloned.1.call-done), kind=kLoop, calls=%fused_computation.75 | loop fusion | bytes 7077888 | tf_op jit(solution)/shard_map/slice | solution.py:26
  99.6 1.1 fusion
  100.7 1.1 fusion.4
  101.8 1.2 add_bitcast_fusion
  103.0 1.2 subtract_bitcast_fusion
  104.1 3.8 pad_maximum_fusion
  108.0 11.3 %copy.55 = f32[576,3,2,512]{3,2,1,0:T(2,128)} copy(f32[576,3,2,512]{3,0,1,2:T(8,128)} %pad_maximum_fusion) | data formatting | bytes 14155776 | tf_op jit(solution)/shard_map/stack | solution.py:30
  119.3 0.0 copy-start.6
  119.3 0.0 all-reduce.5.cloned.1.call-update
  119.3 0.0 all-gather.8.cloned.1.call-start
  119.4 0.8 copy-done.4
  120.2 0.6 copy.57
  120.8 0.0 all-gather.8.cloned.1.call-update
  120.9 0.0 all-reduce.7.cloned.1.call-start
  121.0 0.6 dynamic-slice
  122.3 47.9 %all_gather.12 = bf16[384,2,512]{2,0,1:T(8,128)(2,1)S(1)} all-gather(bf16[24,2,512]{2,0,1:T(8,128)(2,1)S(1)} %copy.46), channel_id=1, replica_groups=mesh['ga'=16,'pair'=16] {'pair'}, dimensions={0}, use_global_device_ids=true | all-gather | bytes 835584 | tf_op jit(solution)/shard_map/all_gather | solution.py:50
  170.2 0.5 fusion.23
  170.7 0.5 fusion.14
  171.2 0.5 fusion.24
  171.7 0.5 fusion.15
  172.1 0.7 pad_maximum_fusion.2
  172.8 170.3 %all-reduce.5.cloned.1.call-done = f32[576,3,2,512]{3,2,1,0:T(2,128)} async-done(((f32[576,3,2,512]{3,2,1,0:T(2,128)}), f32[576,3,2,512]{3,2,1,0:T(2,128)}) %all-reduce.5.cloned.1.call-update) | async-done | bytes 7077904
  343.1 1.6 constant_dynamic-slice_fusion
  344.7 64.8 %all-gather.8.cloned.1.call-done = bf16[256,3,2,512]{3,0,1,2:T(8,128)(2,1)} async-done(((bf16[16,3,2,512]{3,0,1,2:T(8,128)(2,1)}), bf16[256,3,2,512]{3,0,1,2:T(8,128)(2,1)}) %all-gather.8.cloned.1.call-update) | async-done | bytes 1572880 | tf_op jit(solution)/shard_map/all_gather | solution.py:65
  409.5 2.0 fusion.20
  411.6 1.9 fusion.21
  413.5 1.9 fusion.12
  415.5 0.8 fusion.13
  416.2 0.7 pad_maximum_fusion.1
  416.9 0.0 all-reduce.7.cloned.1.call-update
  417.0 146.2 %all-reduce.7.cloned.1.call-done = (f32[384,3,2,24]{0,3,1,2:T(8,128)}, f32[256,3,2,36]{0,3,1,2:T(8,128)}) async-done(((f32[384,3,2,24]{0,3,1,2:T(8,128)}, f32[256,3,2,36]{0,3,1,2:T(8,128)}), (f32[384,3,2,24]{0,3,1,2:T(8,128)}, f32[256,3,2,36]{0,3,1,2:T(8,128)})) %all-reduce.7.cloned.1.call-update) | async-done | bytes 442384 | tf_op jit(solution)/shard_map/psum | solution.py:67
  563.2 1.1 copy.59
  564.2 2.7 stack.55
  566.9 18.8 %all-to-all-start = ((f32[16,256,3,2,36]{1,3,4,2,0:T(2,128)}), f32[16,256,3,2,36]{1,3,4,2,0:T(2,128)S(1)}, u32[]{:S(2)}, u32[]{:S(2)}) async-start(f32[16,256,3,2,36]{1,3,4,2,0:T(2,128)} %stack.55), calls=%async_computation | async-start | bytes 7077888 | tf_op jit(solution)/shard_map/all_to_all | solution.py:70
  585.7 0.0 all-gather.4.cloned.1.call-start
  585.8 0.5 all-gather.4.cloned.1.call-update
  586.3 0.6 fusion.32
  587.0 0.6 copy-done.7
  587.5 0.7 broadcast_add_fusion
  588.2 1.4 add.121
  589.6 0.1 add.129
  589.7 0.6 pad_clamp_fusion.1
  590.3 0.7 fusion.31
  591.0 1.3 fusion.6
  592.3 93.6 %all-to-all-done = f32[16,256,3,2,36]{1,3,4,2,0:T(2,128)S(1)} async-done(((f32[16,256,3,2,36]{1,3,4,2,0:T(2,128)}), f32[16,256,3,2,36]{1,3,4,2,0:T(2,128)S(1)}, u32[]{:S(2)}, u32[]{:S(2)}) %all-to-all-start) | async-done | bytes 3538976 | tf_op jit(solution)/shard_map/all_to_all | solution.py:70
  685.9 3.0 copy.60
  688.8 8.3 %copy.61 = f32[256,3,2,576]{3,1,2,0:T(4,128)} copy(f32[256,3,2,576]{0,2,3,1:T(2,128)} %bitcast.103) | data formatting | bytes 7077888 | tf_op jit(solution)/shard_map/reshape | solution.py:69
  697.2 26.6 %gather_fusion.1 = f32[576,3,2,576]{3,1,2,0:T(4,128)} fusion(f32[256,3,2,576]{3,1,2,0:T(4,128)} %copy.61, s32[1024]{0:T(1024)S(1)} %pad_clamp_fusion), kind=kCustom, calls=%fused_computation.1 | custom fusion | bytes 15927552 | tf_op jit(solution)/shard_map/gather | solution.py:80
  723.8 7.3 multiply_reduce_fusion
  731.1 1.0 copy.63
  732.1 6.2 copy.47
  738.3 1.5 gather_fusion
  739.8 1.5 fusion.17
  741.3 0.7 copy.64
  (24 shorter events, 0.1 us)
Async XLA Ops:
  6.5 83.9 %all-gather.6.cloned.1.call-start = ((), (), s32[]{:S(2)}) async-start(), calls=%async_computation.2 | async-start | bytes 3760128 | tf_op jit(solution)/shard_map/all_gather | solution.py:60
  9.7 89.8 %copy-start = (bf16[3,2,512,512]{3,2,1,0:T(8,128)(2,1)S(1)}, bf16[3,2,512,512]{3,2,1,0:T(8,128)(2,1)}, u32[]{:S(2)}) copy-start(bf16[3,2,512,512]{3,2,1,0:T(8,128)(2,1)} %param.10) | copy-start | bytes 9437188
  9.7 333.4 %all-reduce.5.cloned.1.call-start = ((), (), s32[]{:S(2)}) async-start(), calls=%async_computation.4 | async-start | bytes 14155776
  119.3 0.9 copy-start.4
  119.3 1.6 copy-start.5
  119.3 1.7 copy-start.10
  119.3 2.9 copy-start.3
  119.3 2.9 copy-start.6
  119.3 290.2 %all-gather.8.cloned.1.call-start = ((), (), s32[]{:S(2)}) async-start(), calls=%async_computation.3 | async-start | bytes 1671168 | tf_op jit(solution)/shard_map/all_gather | solution.py:65
  120.9 442.3 %all-reduce.7.cloned.1.call-start = ((), (), s32[]{:S(2)}) async-start(), calls=%async_computation.5 | async-start | bytes 933888 | tf_op jit(solution)/shard_map/psum | solution.py:67
  409.5 5.9 copy-start.1
  566.9 19.4 %copy-start.9 = (s32[384]{0:T(512)S(1)}, s32[384]{0:T(512)}, u32[]{:S(2)}) copy-start(s32[384]{0:T(512)} %param.15) | copy-start | bytes 4612
  566.9 118.9 %all-to-all-start = ((f32[16,256,3,2,36]{1,3,4,2,0:T(2,128)}), f32[16,256,3,2,36]{1,3,4,2,0:T(2,128)S(1)}, u32[]{:S(2)}, u32[]{:S(2)}) async-start(f32[16,256,3,2,36]{1,3,4,2,0:T(2,128)} %stack.55), calls=%async_computation | async-start | bytes 7077888 | tf_op jit(solution)/shard_map/all_to_all | solution.py:70
  585.7 146.4 %all-gather.4.cloned.1.call-start = ((), (), s32[]{:S(2)}) async-start(), calls=%async_computation.1 | async-start | bytes 3760128 | tf_op jit(solution)/shard_map/all_gather | solution.py:72
  587.0 0.6 copy-start.7
  697.2 26.6 %copy-start.2 = (f32[576,576]{1,0:T(8,128)S(1)}, f32[576,576]{1,0:T(8,128)}, u32[]{:S(2)}) copy-start(f32[576,576]{1,0:T(8,128)} %fusion.6) | copy-start | bytes 3981316
  732.1 7.7 %copy-start.8 = (s32[24]{0:T(128)S(1)}, s32[24]{0:T(128)}, u32[]{:S(2)}) copy-start(s32[24]{0:T(128)} %copy-done.7) | copy-start | bytes 292
Sparse Core Ops, SparseCore 0:
  9.8 80.5 all-gather.5
  119.5 223.6 all-reduce.4
  345.9 63.5 all-gather.7
  417.1 146.0 all-reduce.6
  589.0 96.0 all-gather.3
